TPU v7x, 32 devices: a whole 2x2x4 slice. The times are simulated.
32 devices in a mesh: seq: 8 (over z, y), head: 4 (over x, core).
Axes of the slice: x: 2, y: 2, z: 4, core: 2. Of those that a mesh axis runs over, the one named last changes fastest.
Arguments:
- tokens: bfloat16 [1024, 1024], P('seq'), may hold values from -6 to 6
- cotangent: bfloat16 [1024, 1024], P('seq'), may hold values from -6 to 6
- gate_code: int32 [2, 1024, 8], P(None, 'seq', 'head'), may hold values from 0 to 723000
- beta_code: int32 [2, 1024, 8], P(None, 'seq', 'head'), may hold values from 256 to 1024
- norm1_gain: float32 [2, 1024], replicated, may hold values from 0.5 to 1.5
- weight_in: bfloat16 [2, 1024, 6144], P(None, None, 'head'), may hold values from -0.1875 to 0.1875
- conv_weight: bfloat16 [2, 4, 4096], P(None, None, 'head'), may hold values from -3 to 3
- out_gain: float32 [2, 256], replicated, may hold values from 0.5 to 1.5
- weight_out: bfloat16 [2, 2048, 1024], P(None, 'head'), may hold values from -0.25 to 0.25
- norm2_gain: float32 [2, 1024], replicated, may hold values from 0.5 to 1.5
- weight_gate: bfloat16 [2, 1024, 2816], P(None, None, 'head'), may hold values from -0.1875 to 0.1875
- weight_up: bfloat16 [2, 1024, 2816], P(None, None, 'head'), may hold values from -0.1875 to 0.1875
- weight_down: bfloat16 [2, 2816, 1024], P(None, 'head'), may hold values from -0.21875 to 0.21875
Outputs:
- activations: bfloat16 [1024, 1024], P('seq')
- input_grad: float32 [1024, 1024], P('seq')
- grad_norm1_gain: float32 [2, 1024], replicated
- grad_weight_in: float32 [2, 1024, 6144], P(None, 'seq', 'head')
- grad_conv_weight: float32 [2, 4, 4096], P(None, None, 'head')
- grad_out_gain: float32 [2, 256], replicated
- grad_weight_out: float32 [2, 2048, 1024], P(None, 'head', 'seq')
- grad_norm2_gain: float32 [2, 1024], replicated
- grad_weight_gate: float32 [2, 1024, 2816], P(None, 'seq', 'head')
- grad_weight_up: float32 [2, 1024, 2816], P(None, 'seq', 'head')
- grad_weight_down: float32 [2, 2816, 1024], P(None, 'head', 'seq')
All inputs are finite; a program needn't handle non-finite values.
Results may differ from a plain program's by a relative error of at most 0.02.
Values sent between devices are 32-bit elements; how exact they have to be, the bound alone decides.
No kernel may reach another device: no remote copies, remote signals or barrier semaphores. Data moves between devices by JAX's collectives and lax.ppermute only.
A program may use at most 256 MiB of HBM per device.

v0:
```python
import jax
import jax.numpy as jnp
from jax import lax
from jax.sharding import PartitionSpec as P

DK = 128
DV = 256
CONV = 4
SPAN = 64
STACK_LEVELS = 2
highest = lax.Precision.HIGHEST
norm_eps = 1e-06
gate_unit = 1.0 / 1048576.0
beta_unit = 1.0 / 1024.0


def from_behind(array, axis, by):
    length = lax.axis_size(axis)
    pairs = [(i, i + by) for i in range(length) if 0 <= i + by < length]
    return lax.ppermute(array, axis, pairs)


def rms_norm(stream, gain):
    return stream * lax.rsqrt(jnp.mean(stream * stream, axis=-1, keepdims=True) + norm_eps) * gain


def unit_rows(vectors):
    return vectors * lax.rsqrt(jnp.sum(vectors * vectors, axis=-1, keepdims=True) + norm_eps)


def swiglu(gate_pre, up_pre):
    return jax.nn.silu(gate_pre) * up_pre


def post_mix(outputs, gate_z, gain):
    return rms_norm(outputs, gain) * jax.nn.silu(gate_z)


def mixer_inputs(windowed, conv_taps):
    length_total = windowed.shape[0] - (CONV - 1)
    conv_out = conv_taps[0] * windowed[CONV - 1 :]
    for tap_index in range(1, CONV):
        conv_out = (
            conv_out
            + conv_taps[tap_index]
            * windowed[CONV - 1 - tap_index : CONV - 1 - tap_index + length_total]
        )
    active = jax.nn.silu(conv_out).reshape(length_total, -1, 2 * DK + DV)
    queries = unit_rows(active[:, :, :DK]) * DK ** (-0.5)
    keys_unit = unit_rows(active[:, :, DK : 2 * DK])
    return (queries, keys_unit, active[:, :, 2 * DK :])


def span_step(carry_state, pieces):
    queries, keys_unit, values_in, logdecay, beta_rate = pieces
    block_len = queries.shape[0]
    cumulated = jnp.cumsum(logdecay, axis=0)
    cum_heads = jnp.transpose(cumulated)
    row_index = lax.broadcasted_iota(jnp.int32, (1, block_len, block_len), 1)
    col_index = lax.broadcasted_iota(jnp.int32, (1, block_len, block_len), 2)
    inclusive = row_index >= col_index
    log_ratio = jnp.where(inclusive, cum_heads[:, :, None] - cum_heads[:, None, :], 0.0)
    decay_ratio = jnp.where(inclusive, jnp.exp(log_ratio), 0.0)
    beta_heads = jnp.transpose(beta_rate)
    key_key = jnp.einsum("thd,shd->hts", keys_unit, keys_unit, precision=highest)
    strict_lower = jnp.where(
        row_index > col_index, beta_heads[:, :, None] * decay_ratio * key_key, 0.0
    )
    system = strict_lower + jnp.eye(block_len, dtype=strict_lower.dtype)[None]
    decay_all = jnp.exp(cumulated)
    right_side = jnp.concatenate(
        [beta_rate[:, :, None] * values_in, (beta_rate * decay_all)[:, :, None] * keys_unit], axis=2
    )
    right_side = jnp.transpose(right_side, (1, 0, 2))
    solved_system = lax.linalg.triangular_solve(system, right_side, left_side=True, lower=True)
    val_width = values_in.shape[2]
    new_values = solved_system[:, :, :val_width] - jnp.einsum(
        "htd,hvd->htv", solved_system[:, :, val_width:], carry_state, precision=highest
    )
    query_key = jnp.einsum("thd,shd->hts", queries, keys_unit, precision=highest)
    mixing = decay_ratio * query_key
    outputs = jnp.transpose(decay_all)[:, :, None] * jnp.einsum(
        "thd,hvd->htv", queries, carry_state, precision=highest
    )
    outputs = outputs + jnp.einsum("hts,hsv->htv", mixing, new_values, precision=highest)
    to_end = jnp.exp(cumulated[-1][None, :] - cumulated)
    new_state = jnp.exp(cumulated[-1])[:, None, None] * carry_state
    new_state = new_state + jnp.einsum(
        "hsv,shd->hvd", new_values, to_end[:, :, None] * keys_unit, precision=highest
    )
    return (new_state, jnp.transpose(outputs, (1, 0, 2)))


def delta_rule(queries, keys_unit, values_in, logdecay, beta_rate, carry_state):
    length_total = queries.shape[0]
    block_count = length_total // SPAN

    def blocks(tensor):
        return tensor.reshape((block_count, SPAN) + tensor.shape[1:])

    final_state, outputs = lax.scan(
        span_step,
        carry_state,
        (
            blocks(queries),
            blocks(keys_unit),
            blocks(values_in),
            blocks(logdecay),
            blocks(beta_rate),
        ),
    )
    return (outputs.reshape((length_total,) + outputs.shape[2:]), final_state)


def state_prefix(transfer, offset):
    all_transfer, all_offset = (
        lax.all_gather(transfer, "seq", axis=0, tiled=True),
        lax.all_gather(offset, "seq", axis=0, tiled=True),
    )
    devices = lax.axis_size("seq")
    position = lax.axis_index("seq")
    transfer_kept = all_transfer.reshape((devices,) + transfer.shape)
    offsets_all = all_offset.reshape((devices,) + offset.shape)

    def advance(index_now, carry_state):
        moved = (
            jnp.einsum("hvj,hjk->hvk", carry_state, transfer_kept[index_now], precision=highest)
            + offsets_all[index_now]
        )
        return jnp.where(index_now < position, moved, carry_state)

    incoming = lax.fori_loop(0, devices, advance, jnp.zeros_like(offset))
    return (incoming, transfer_kept)


def state_back(transfer_kept, local_grad):
    all_grad = lax.all_gather(local_grad, "seq", axis=0, tiled=True)
    devices = lax.axis_size("seq")
    position = lax.axis_index("seq")
    grads_all = all_grad.reshape((devices,) + local_grad.shape)

    def retreat(step_index, carry_state):
        index_now = devices - 1 - step_index
        moved = (
            jnp.einsum("hvj,hkj->hvk", carry_state, transfer_kept[index_now], precision=highest)
            + grads_all[index_now]
        )
        return jnp.where(index_now > position, moved, carry_state)

    outgoing = lax.fori_loop(0, devices, retreat, jnp.zeros_like(local_grad))
    return outgoing


def head_total(partial_sum):
    share = lax.psum_scatter(partial_sum, "head", scatter_dimension=1, tiled=True)
    return lax.all_gather(share, "head", axis=1, tiled=True)


def layer_forward(stream, logdecay, beta_rate, weights):
    (
        gain_one,
        weight_in,
        conv_weight,
        out_gain,
        weight_out,
        gain_two,
        weight_gate,
        weight_up,
        weight_down,
    ) = weights
    length_total = stream.shape[0]
    normed = rms_norm(stream, gain_one).astype(jnp.bfloat16)
    projected = jnp.dot(normed, weight_in, preferred_element_type=jnp.float32).reshape(
        length_total, -1, 2 * DK + 2 * DV
    )
    head_count = projected.shape[1]
    conv_input = projected[:, :, : 2 * DK + DV].reshape(length_total, -1)
    gate_z = projected[:, :, 2 * DK + DV :]
    before = from_behind(conv_input[length_total - (CONV - 1) :], "seq", 1)
    windowed = jnp.concatenate([before, conv_input], axis=0)
    conv_taps = conv_weight.astype(jnp.float32)
    queries, keys_unit, values_in = mixer_inputs(windowed, conv_taps)
    wide_values = jnp.concatenate(
        [values_in, jnp.zeros((length_total, head_count, DK), jnp.float32)], axis=2
    )
    start_state = jnp.concatenate(
        [
            jnp.zeros((head_count, DV, DK), jnp.float32),
            jnp.broadcast_to(jnp.eye(DK, dtype=jnp.float32), (head_count, DK, DK)),
        ],
        axis=1,
    )
    wide_out, wide_end = delta_rule(
        queries, keys_unit, wide_values, logdecay, beta_rate, start_state
    )
    carried = wide_out[:, :, DV:]
    incoming, transfer_kept = state_prefix(wide_end[:, DV:], wide_end[:, :DV])
    outputs = wide_out[:, :, :DV] + jnp.einsum("thd,hvd->thv", carried, incoming, precision=highest)
    gated_out = post_mix(outputs, gate_z, out_gain).reshape(length_total, -1).astype(jnp.bfloat16)
    stream_mid = stream + head_total(
        jnp.dot(gated_out, weight_out, preferred_element_type=jnp.float32)
    )
    second_normed = rms_norm(stream_mid, gain_two).astype(jnp.bfloat16)
    gate_pre = jnp.dot(second_normed, weight_gate, preferred_element_type=jnp.float32)
    up_pre = jnp.dot(second_normed, weight_up, preferred_element_type=jnp.float32)
    hidden = swiglu(gate_pre, up_pre).astype(jnp.bfloat16)
    stream_next = stream_mid + head_total(
        jnp.dot(hidden, weight_down, preferred_element_type=jnp.float32)
    )
    stored = (
        stream,
        normed,
        windowed,
        conv_taps,
        gate_z,
        queries,
        keys_unit,
        values_in,
        outputs,
        carried,
        incoming,
        transfer_kept,
        gated_out,
        stream_mid,
        second_normed,
        gate_pre,
        up_pre,
        hidden,
    )
    return (stream_next, stored)


def layer_backward(grad_stream, logdecay, beta_rate, weights, stored):
    (
        gain_one,
        weight_in,
        conv_weight,
        out_gain,
        weight_out,
        gain_two,
        weight_gate,
        weight_up,
        weight_down,
    ) = weights
    (
        stream,
        normed,
        windowed,
        conv_taps,
        gate_z,
        queries,
        keys_unit,
        values_in,
        outputs,
        carried,
        incoming,
        transfer_kept,
        gated_out,
        stream_mid,
        second_normed,
        gate_pre,
        up_pre,
        hidden,
    ) = stored
    length_total = grad_stream.shape[0]
    back_bf = grad_stream.astype(jnp.bfloat16)
    grad_down = jnp.dot(hidden.T, back_bf, preferred_element_type=jnp.float32)
    grad_hidden = jnp.dot(back_bf, weight_down.T, preferred_element_type=jnp.float32)
    _, act_pull = jax.vjp(swiglu, gate_pre, up_pre)
    grad_gate_pre, grad_up_pre = act_pull(grad_hidden)
    grad_gate_pre = grad_gate_pre.astype(jnp.bfloat16)
    grad_up_pre = grad_up_pre.astype(jnp.bfloat16)
    grad_gate = jnp.dot(second_normed.T, grad_gate_pre, preferred_element_type=jnp.float32)
    grad_up = jnp.dot(second_normed.T, grad_up_pre, preferred_element_type=jnp.float32)
    ffn_partial = jnp.dot(
        grad_gate_pre, weight_gate.T, preferred_element_type=jnp.float32
    ) + jnp.dot(grad_up_pre, weight_up.T, preferred_element_type=jnp.float32)
    grad_normed_two = lax.psum(ffn_partial, "head")
    _, norm_pull = jax.vjp(rms_norm, stream_mid, gain_two)
    grad_mid, grad_gain_two = norm_pull(grad_normed_two)
    grad_stream = grad_stream + grad_mid
    back_bf = grad_stream.astype(jnp.bfloat16)
    grad_out = jnp.dot(gated_out.T, back_bf, preferred_element_type=jnp.float32)
    grad_gated = jnp.dot(back_bf, weight_out.T, preferred_element_type=jnp.float32).reshape(
        length_total, -1, DV
    )
    _, post_pull = jax.vjp(post_mix, outputs, gate_z, out_gain)
    grad_outputs, grad_gate_z, gain_mid_part = post_pull(grad_gated)
    local_grad = jnp.einsum("thv,thd->hvd", grad_outputs, carried, precision=highest)
    outgoing = state_back(transfer_kept, local_grad)

    def core_rule(queries, keys_unit, values_in):
        return delta_rule(queries, keys_unit, values_in, logdecay, beta_rate, incoming)

    _, rule_pull = jax.vjp(core_rule, queries, keys_unit, values_in)
    grad_queries, grad_keys, grad_values = rule_pull((grad_outputs, outgoing))
    _, mix_pull = jax.vjp(mixer_inputs, windowed, conv_taps)
    grad_window, grad_conv = mix_pull((grad_queries, grad_keys, grad_values))
    from_next = from_behind(grad_window[: CONV - 1], "seq", -1)
    grad_conv_in = grad_window[CONV - 1 :] + jnp.pad(
        from_next, ((length_total - (CONV - 1), 0), (0, 0))
    )
    grad_proj = (
        jnp.concatenate([grad_conv_in.reshape(length_total, -1, 2 * DK + DV), grad_gate_z], axis=2)
        .reshape(length_total, -1)
        .astype(jnp.bfloat16)
    )
    grad_in = jnp.dot(normed.T, grad_proj, preferred_element_type=jnp.float32)
    mixer_partial = jnp.dot(grad_proj, weight_in.T, preferred_element_type=jnp.float32)
    grad_normed, grad_out_gain = lax.psum((mixer_partial, gain_mid_part), "head")
    _, norm_pull = jax.vjp(rms_norm, stream, gain_one)
    grad_prev, grad_gain_one = norm_pull(grad_normed)
    return (
        grad_stream + grad_prev,
        (
            grad_gain_one,
            grad_in,
            grad_conv,
            grad_out_gain,
            grad_out,
            grad_gain_two,
            grad_gate,
            grad_up,
            grad_down,
        ),
    )


def body(
    tokens,
    cotangent,
    gate_code,
    beta_code,
    norm1_gain,
    weight_in,
    conv_weight,
    out_gain,
    weight_out,
    norm2_gain,
    weight_gate,
    weight_up,
    weight_down,
):
    logdecay = -gate_code.astype(jnp.float32) * gate_unit
    beta_rate = beta_code.astype(jnp.float32) * beta_unit
    everything = (
        norm1_gain,
        weight_in,
        conv_weight,
        out_gain,
        weight_out,
        norm2_gain,
        weight_gate,
        weight_up,
        weight_down,
    )
    stream = tokens.astype(jnp.float32)
    kept_layers = []
    for layer_idx in range(STACK_LEVELS):
        weights = tuple((tensor[layer_idx] for tensor in everything))
        stream, stored = layer_forward(stream, logdecay[layer_idx], beta_rate[layer_idx], weights)
        kept_layers.append((weights, stored))
    activations = stream.astype(jnp.bfloat16)
    grad_stream = cotangent.astype(jnp.float32)
    large_grads = []
    small_grads = []
    for layer_idx in reversed(range(STACK_LEVELS)):
        weights, stored = kept_layers[layer_idx]
        grad_stream, layer_part = layer_backward(
            grad_stream, logdecay[layer_idx], beta_rate[layer_idx], weights, stored
        )
        large_part = (layer_part[1], layer_part[4], layer_part[6], layer_part[7], layer_part[8])
        large_grads.insert(0, large_part)
        small_grads.insert(0, (layer_part[2], layer_part[0], layer_part[3], layer_part[5]))
    large_stack = tuple(
        (
            jnp.stack([grad_group[slot_index] for grad_group in large_grads])
            for slot_index in range(5)
        )
    )
    large_stack = (
        lax.psum_scatter(large_stack[0], "seq", scatter_dimension=1, tiled=True),
        lax.psum_scatter(large_stack[1], "seq", scatter_dimension=2, tiled=True),
        lax.psum_scatter(large_stack[2], "seq", scatter_dimension=1, tiled=True),
        lax.psum_scatter(large_stack[3], "seq", scatter_dimension=1, tiled=True),
        lax.psum_scatter(large_stack[4], "seq", scatter_dimension=2, tiled=True),
    )
    small_stack = tuple(
        (
            jnp.stack([grad_group[slot_index] for grad_group in small_grads])
            for slot_index in range(4)
        )
    )
    conv_grad, gain_one_grad, out_gain_grad, gain_two_grad = lax.psum(
        (small_stack[0], small_stack[1], small_stack[2], small_stack[3]), "seq"
    )
    return (
        activations,
        grad_stream,
        gain_one_grad,
        large_stack[0],
        conv_grad,
        out_gain_grad,
        large_stack[1],
        gain_two_grad,
        large_stack[2],
        large_stack[3],
        large_stack[4],
    )


def solution(mesh):
    in_specs = (
        P("seq", None),
        P("seq", None),
        P(None, "seq", "head"),
        P(None, "seq", "head"),
        P(),
        P(None, None, "head"),
        P(None, None, "head"),
        P(),
        P(None, "head", None),
        P(),
        P(None, None, "head"),
        P(None, None, "head"),
        P(None, "head", None),
    )
    out_specs = (
        P("seq", None),
        P("seq", None),
        P(),
        P(None, "seq", "head"),
        P(None, None, "head"),
        P(),
        P(None, "head", "seq"),
        P(),
        P(None, "seq", "head"),
        P(None, "seq", "head"),
        P(None, "head", "seq"),
    )
    return jax.shard_map(body, mesh=mesh, in_specs=in_specs, out_specs=out_specs, check_vma=False)
```

profile of v0, /device:TPU:0, one launch (start us, length us, event | category | flops | bytes accessed | tf_op | source)
XLA Modules:
  0.0 1594.9 jit_solution(10691709195272504350)
XLA Ops:
  26.3 10.4 collective-permute-done
  41.2 28.4 %while.210 = (s32[]{:T(128)}, f32[2,384,128]{2,1,0:T(8,128)S(1)}, f32[2,64,2,384]{3,1,0,2:T(8,128)S(1)}, f32[2,64,2]{1,2,0:T(2,128)S(1)}, f32[2,64,2]{1,2,0:T(2,...) while((s32[]{:T(128)}, f32[2,384,128]{2,1,0:T(8,128)S(1)}, ...), condition=%wide.region_5.7_spmd, body=%wide.region_3.6_spmd.sunk | while | flops 340353152 | bytes 4627117 | solution.py:101
  71.3 41.7 %all-gather.7.cloned.1.call-done = f32[16,128,128]{2,1,0:T(8,128)} async-done(((f32[2,128,128]{2,1,0:T(8,128)}), f32[16,128,128]{2,1,0:T(8,128)}) %all-gather.7.cloned.1.call-update) | async-done | bytes 1048592 | tf_op jit(solution)/shard_map/all_gather | solution.py:117
  113.0 50.5 %all-gather.9.cloned.1.call-done = f32[16,256,128]{2,1,0:T(8,128)} async-done(((f32[2,256,128]{2,1,0:T(8,128)}), f32[16,256,128]{2,1,0:T(8,128)}) %all-gather.9.cloned.1.call-update) | async-done | bytes 2097168 | tf_op jit(solution)/shard_map/all_gather | solution.py:118
  163.5 20.1 %while.216 = (s32[]{:T(128)}, f32[2,256,128]{1,2,0:T(8,128)S(1)}, s32[]{:T(128)}, f32[8,2,128,128]{3,2,1,0:T(8,128)}, f32[8,2,256,128]{3,2,1,0:T(8,128)}, /*index=5*/s32[]{:T(128)}, s32[]{:T(128)}) while((s32[]{:T(128)}, f32[2,256,128]{1,2,0:T(8,128)S(1)}, s32[]{:T(128)}, f32[8,2,128,128]{3,2,1,0:T(8,128)}, ...), condition=%wide.region_7.9_spmd.clone, body=%wide.region_6.8_spmd.clone.sunk | while | flops 100925440 | bytes 2754667 | solution.py:132
  187.0 20.2 %reduce-scatter.10.cloned.1.call-done = f32[128,256]{1,0:T(8,128)} async-done(((f32[128,1024]{1,0:T(8,128)}), f32[128,256]{1,0:T(8,128)}) %reduce-scatter.10.cloned.1.call-update) | async-done | bytes 131088 | tf_op jit(solution)/shard_map/reduce_scatter | solution.py:155
  223.9 17.5 %reduce-scatter.12.cloned.1.call-done = f32[128,256]{1,0:T(8,128)} async-done(((f32[128,1024]{1,0:T(8,128)}), f32[128,256]{1,0:T(8,128)}) %reduce-scatter.12.cloned.1.call-update) | async-done | bytes 131088 | tf_op jit(solution)/shard_map/reduce_scatter | solution.py:155
  275.9 30.3 %while.211 = (s32[]{:T(128)}, f32[2,384,128]{2,1,0:T(8,128)S(1)}, f32[2,64,2,384]{3,1,0,2:T(8,128)S(1)}, f32[2,64,2]{1,2,0:T(2,128)S(1)}, f32[2,64,2]{1,2,0:T(2,...) while((s32[]{:T(128)}, f32[2,384,128]{2,1,0:T(8,128)S(1)}, ...), condition=%wide.region_17.19_spmd, body=%wide.region_15.18_spmd.sunk | while | flops 340353152 | bytes 4627117 | solution.py:101
  307.8 41.1 %all-gather.11.cloned.1.call-done = f32[16,128,128]{2,1,0:T(8,128)} async-done(((f32[2,128,128]{2,1,0:T(8,128)}), f32[16,128,128]{2,1,0:T(8,128)}) %all-gather.11.cloned.1.call-update) | async-done | bytes 1048592 | tf_op jit(solution)/shard_map/all_gather | solution.py:117
  348.9 50.4 %all-gather.13.cloned.1.call-done = f32[16,256,128]{2,1,0:T(8,128)} async-done(((f32[2,256,128]{2,1,0:T(8,128)}), f32[16,256,128]{2,1,0:T(8,128)}) %all-gather.13.cloned.1.call-update) | async-done | bytes 2097168 | tf_op jit(solution)/shard_map/all_gather | solution.py:118
  399.3 20.0 %while.217 = (s32[]{:T(128)}, f32[2,256,128]{1,2,0:T(8,128)S(1)}, s32[]{:T(128)}, f32[8,2,128,128]{3,2,1,0:T(8,128)}, f32[8,2,256,128]{3,2,1,0:T(8,128)}, /*index=5*/s32[]{:T(128)}, s32[]{:T(128)}) while((s32[]{:T(128)}, f32[2,256,128]{1,2,0:T(8,128)S(1)}, s32[]{:T(128)}, f32[8,2,128,128]{3,2,1,0:T(8,128)}, ...), condition=%wide.region_19.21_spmd.clone, body=%wide.region_18.20_spmd.clone.sunk | while | flops 100925440 | bytes 2754667 | solution.py:132
  426.3 17.6 %reduce-scatter.14.cloned.1.call-done = f32[128,256]{1,0:T(8,128)} async-done(((f32[128,1024]{1,0:T(8,128)}), f32[128,256]{1,0:T(8,128)}) %reduce-scatter.14.cloned.1.call-update) | async-done | bytes 131088 | tf_op jit(solution)/shard_map/reduce_scatter | solution.py:155
  462.5 28.1 %all-reduce.38.cloned.1.call-done = f32[128,1024]{1,0:T(8,128)} async-done(((f32[128,1024]{1,0:T(8,128)}), f32[128,1024]{1,0:T(8,128)}) %all-reduce.38.cloned.1.call-update) | async-done | bytes 524304 | tf_op jit(solution)/shard_map/psum | solution.py:278
  492.4 23.1 %reduce-scatter.16.cloned.1.call-done = f32[128,256]{1,0:T(8,128)} async-done(((f32[128,1024]{1,0:T(8,128)}), f32[128,256]{1,0:T(8,128)}) %reduce-scatter.16.cloned.1.call-update) | async-done | bytes 131088 | tf_op jit(solution)/shard_map/reduce_scatter | solution.py:155
  535.7 39.1 %while.214 = (s32[]{:T(128)}, f32[2,256,128]{2,1,0:T(8,128)S(1)}, f32[2,2,64,64]{3,2,1,0:T(8,128)}, f32[2,64,2,1]{1,2,3,0:T(2,128)S(1)}, f32[2,64,2,1]{1,2,3,0:T...) while((s32[]{:T(128)}, f32[2,256,128]{2,1,0:T(8,128)S(1)}, ...), condition=%wide.region_31.34_spmd.clone.clone, body=%wide.region_29.33_spmd.clone.clone.sunk | while | flops 164024704 | bytes 3933053 | solution.py:101
  541.2 9.9 custom-call.38
  579.9 32.3 %while.218 = (s32[]{:T(128)}, f32[2,256,128]{1,2,0:T(8,128)}, s32[]{:T(128)}, f32[8,2,128,128]{3,2,1,0:T(8,128)}, f32[8,2,256,128]{3,2,1,0:T(8,128)}, /*index=5*/s32[]{:T(128)}, s32[]{:T(128)}, s32[]{:T(128)}, s32[]{:T(128)}) while((s32[]{:T(128)}, f32[2,256,128]{1,2,0:T(8,128)}, s32[]{:T(128)}, f32[8,2,128,128]{3,2,1,0:T(8,128)}, ...), condition=%wide.region_28.30_spmd.clone, body=%wide.region_27.29_spmd.clone.sunk | while | flops 100925448 | bytes 2754729 | solution.py:150
  615.2 43.8 %while.212 = (s32[]{:T(128)}, f32[2,256,128]{2,1,0:T(8,128)S(1)}, f32[2,64,2,128]{3,1,0,2:T(8,128)}, f32[2,64,2,128]{3,1,0,2:T(8,128)}, f32[2,64,2,256]{3,1,0,2:...) while((s32[]{:T(128)}, f32[2,256,128]{2,1,0:T(8,128)S(1)}, ...), condition=%wide.region_33.38_spmd.clone, body=%wide.region_32.37_spmd.clone.sunk | while | flops 485101568 | bytes 11272125 | solution.py:101
  673.0 12.7 collective-permute-done.2
  690.9 33.6 %all-reduce.40.cloned.1.call-done = f32[128,1024]{1,0:T(8,128)} async-done(((f32[128,1024]{1,0:T(8,128)}), f32[128,1024]{1,0:T(8,128)}) %all-reduce.40.cloned.1.call-update) | async-done | bytes 524304 | tf_op jit(solution)/shard_map/psum | solution.py:310
  731.5 33.5 %all-reduce.42.cloned.1.call-done = f32[128,1024]{1,0:T(8,128)} async-done(((f32[128,1024]{1,0:T(8,128)}), f32[128,1024]{1,0:T(8,128)}) %all-reduce.42.cloned.1.call-update) | async-done | bytes 524304 | tf_op jit(solution)/shard_map/psum | solution.py:278
  775.5 33.5 %while.215 = (s32[]{:T(128)}, f32[2,256,128]{2,1,0:T(8,128)S(1)}, f32[2,2,64,64]{3,2,1,0:T(8,128)S(1)}, f32[2,64,2,1]{1,2,3,0:T(2,128)S(1)}, f32[2,64,2,1]{1,2,3...) while((s32[]{:T(128)}, f32[2,256,128]{2,1,0:T(8,128)S(1)}, ...), condition=%wide.region_45.50_spmd.clone.clone, body=%wide.region_43.49_spmd.clone.clone.sunk | while | flops 164024704 | bytes 3990809 | solution.py:101
  809.0 14.1 all-gather.17.cloned.1.call-done
  823.1 19.6 %while.219 = (s32[]{:T(128)}, f32[2,256,128]{1,2,0:T(8,128)S(1)}, s32[]{:T(128)}, f32[8,2,128,128]{3,2,1,0:T(8,128)}, f32[8,2,256,128]{3,2,1,0:T(8,128)}, /*index=5*/s32[]{:T(128)}, s32[]{:T(128)}, s32[]{:T(128)}, s32[]{:T(128)}) while((s32[]{:T(128)}, f32[2,256,128]{1,2,0:T(8,128)S(1)}, s32[]{:T(128)}, ...), condition=%wide.region_42.47_spmd.clone, body=%wide.region_41.46_spmd.clone.sunk | while | flops 100925448 | bytes 2754729 | solution.py:150
  843.7 35.4 %while.213 = (s32[]{:T(128)}, f32[2,256,128]{2,1,0:T(8,128)S(1)}, f32[2,64,2,128]{3,1,0,2:T(8,128)S(1)}, f32[2,64,2,128]{3,1,0,2:T(8,128)S(1)}, f32[2,64,2,256]{...) while((s32[]{:T(128)}, f32[2,256,128]{2,1,0:T(8,128)S(1)}, ...), condition=%wide.region_47.52_spmd.clone, body=%wide.region_46.51_spmd.clone.sunk | while | flops 485101568 | bytes 8618345 | solution.py:101
  886.8 11.9 collective-permute-done.3
  945.9 38.6 %all-reduce.31 = (f32[2,1024]{1,0:T(2,128)}, f32[2,4,1024]{2,1,0:T(4,128)}, f32[2,256]{1,0:T(2,128)}, f32[2,1024]{1,0:T(2,128)}) all-reduce(f32[2,1024]{1,0:T(2,128)S(1)} %pad_maximum_fusion.8, f32[2,4,1024]{2,1,0:T(4,128)S(1)} %pad_maximum_fusion.7, ...), channel_id=1, replica_groups=mesh['seq'=8,'head'=4] {'seq'}, use_global_device_ids=true, to_apply=%region_54.59 | all-reduce | flops 12800 | bytes 102400 | tf_op jit(solution)/shard_map/psum | solution.py:394
  986.5 46.7 %reduce-scatter.20.cloned.1.call-done = f32[2,512,128]{2,1,0:T(8,128)} async-done(((f32[2,512,1024]{2,1,0:T(8,128)}), f32[2,512,128]{2,1,0:T(8,128)}) %reduce-scatter.20.cloned.1.call-update) | async-done | bytes 524304 | tf_op jit(solution)/shard_map/reduce_scatter | solution.py:383
  1033.2 114.8 %reduce-scatter.26.cloned.1.call-done = f32[2,704,128]{2,1,0:T(8,128)} async-done(((f32[2,704,1024]{2,1,0:T(8,128)}), f32[2,704,128]{2,1,0:T(8,128)}) %reduce-scatter.26.cloned.1.call-update) | async-done | bytes 720912 | tf_op jit(solution)/shard_map/reduce_scatter | solution.py:386
  1148.0 114.5 %reduce-scatter.22.cloned.1.call-done = f32[2,128,704]{1,2,0:T(8,128)} async-done(((f32[2,1024,704]{1,2,0:T(8,128)}), f32[2,128,704]{1,2,0:T(8,128)}) %reduce-scatter.22.cloned.1.call-update) | async-done | bytes 720912 | tf_op jit(solution)/shard_map/reduce_scatter | solution.py:384
  1262.5 114.5 %reduce-scatter.24.cloned.1.call-done = f32[2,128,704]{1,2,0:T(8,128)} async-done(((f32[2,1024,704]{1,2,0:T(8,128)}), f32[2,128,704]{1,2,0:T(8,128)}) %reduce-scatter.24.cloned.1.call-update) | async-done | bytes 720912 | tf_op jit(solution)/shard_map/reduce_scatter | solution.py:385
  1377.0 211.0 %reduce-scatter.18.cloned.1.call-done = f32[2,128,1536]{2,1,0:T(8,128)} async-done(((f32[2,1024,1536]{2,1,0:T(8,128)}), f32[2,128,1536]{2,1,0:T(8,128)}) %reduce-scatter.18.cloned.1.call-update) | async-done | bytes 1572880 | tf_op jit(solution)/shard_map/reduce_scatter | solution.py:382
  (1071 shorter events, 518.6 us)
Async XLA Ops:
  7.2 105.8 %all-gather.7.cloned.1.call-start = ((), (), s32[]{:S(2)}) async-start(), calls=%async_computation.9 | async-start | bytes 1179648 | tf_op jit(solution)/shard_map/all_gather | solution.py:117
  9.1 239.5 %copy-start.80 = (f32[1,1024]{1,0:T(1,128)}, f32[1,1024]{1,0:T(1,128)S(1)}, u32[]{:S(2)}) copy-start(f32[1,1024]{1,0:T(1,128)S(1)} %get-tuple-element.3506) | copy-start | bytes 12292
  20.6 16.1 %collective-permute-start = (f32[3,1024]{0,1:T(8,128)S(1)}, f32[3,1024]{0,1:T(8,128)S(1)}, u32[]{:S(2)}, u32[]{:S(2)}) collective-permute-start(f32[3,1024]{0,1:T(8,128)S(1)} %copy.512), channel_id=1, source_target_pairs={{0,4},{4,8},{8,12},{12,16},{16,20},{20,24},{24,28},{1,5},{5,9},{9,... | collective-permute-start | bytes 36872 | tf_op jit(solution)/shard_map/ppermute | solution.py:20
  25.7 243.9 %copy-start.102 = (f32[1,1,1024]{2,1,0:T(1,128)}, f32[1,1,1024]{2,1,0:T(1,128)S(1)}, u32[]{:S(2)}) copy-start(f32[1,1,1024]{2,1,0:T(1,128)S(1)} %get-tuple-element.3494) | copy-start | bytes 12292
  25.7 243.9 %copy-start.104 = (f32[1,1,1024]{2,1,0:T(1,128)}, f32[1,1,1024]{2,1,0:T(1,128)S(1)}, u32[]{:S(2)}) copy-start(f32[1,1,1024]{2,1,0:T(1,128)S(1)} %get-tuple-element.3495) | copy-start | bytes 12292
  25.7 243.9 %copy-start.106 = (f32[1,1,1024]{2,1,0:T(1,128)}, f32[1,1,1024]{2,1,0:T(1,128)S(1)}, u32[]{:S(2)}) copy-start(f32[1,1,1024]{2,1,0:T(1,128)S(1)} %get-tuple-element.3496) | copy-start | bytes 12292
  25.8 243.9 %copy-start.108 = (f32[1,1,1024]{2,1,0:T(1,128)}, f32[1,1,1024]{2,1,0:T(1,128)S(1)}, u32[]{:S(2)}) copy-start(f32[1,1,1024]{2,1,0:T(1,128)S(1)} %get-tuple-element.3497) | copy-start | bytes 12292
  69.6 114.1 %copy-start.57 = (f32[2,64,2,384]{3,1,0,2:T(8,128)}, f32[2,64,2,384]{3,1,0,2:T(8,128)S(1)}, u32[]{:S(2)}) copy-start(f32[2,64,2,384]{3,1,0,2:T(8,128)S(1)} %get-tuple-element.2055) | copy-start | bytes 1179652
  70.4 93.2 %all-gather.9.cloned.1.call-start = ((), (), s32[]{:S(2)}) async-start(), calls=%async_computation.10 | async-start | bytes 2359296 | tf_op jit(solution)/shard_map/all_gather | solution.py:118
  71.1 136.0 %reduce-scatter.10.cloned.1.call-start = ((), (), s32[]{:S(2)}) async-start(), calls=%async_computation.11 | async-start | bytes 655360 | tf_op jit(solution)/shard_map/reduce_scatter | solution.py:155
  71.2 348.6 %copy-start.122 = (f32[1,256]{1,0:T(1,128)}, f32[1,256]{1,0:T(1,128)S(1)}, u32[]{:S(2)}) copy-start(f32[1,256]{1,0:T(1,128)S(1)} %get-tuple-element.3508) | copy-start | bytes 3076
  186.9 54.5 %reduce-scatter.12.cloned.1.call-start = ((), (), s32[]{:S(2)}) async-start(), calls=%async_computation.12 | async-start | bytes 655360 | tf_op jit(solution)/shard_map/reduce_scatter | solution.py:155
  187.0 264.0 %copy-start.92 = (f32[1,1024]{1,0:T(1,128)}, f32[1,1024]{1,0:T(1,128)S(1)}, u32[]{:S(2)}) copy-start(f32[1,1024]{1,0:T(1,128)S(1)} %get-tuple-element.3504) | copy-start | bytes 12292
  219.1 129.8 %all-gather.11.cloned.1.call-start = ((), (), s32[]{:S(2)}) async-start(), calls=%async_computation.13 | async-start | bytes 1179648 | tf_op jit(solution)/shard_map/all_gather | solution.py:117
  248.6 477.8 %copy-start = (f32[128,1024]{1,0:T(8,128)}, f32[128,1024]{1,0:T(8,128)S(1)}, u32[]{:S(2)}) copy-start(f32[128,1024]{1,0:T(8,128)S(1)} %get-tuple-element.3414) | copy-start | bytes 1572868
  254.3 15.4 collective-permute-start.1
  306.9 92.4 %all-gather.13.cloned.1.call-start = ((), (), s32[]{:S(2)}) async-start(), calls=%async_computation.14 | async-start | bytes 2359296 | tf_op jit(solution)/shard_map/all_gather | solution.py:118
  307.7 136.2 %reduce-scatter.14.cloned.1.call-start = ((), (), s32[]{:S(2)}) async-start(), calls=%async_computation.15 | async-start | bytes 655360 | tf_op jit(solution)/shard_map/reduce_scatter | solution.py:155
  423.6 67.0 %all-reduce.38.cloned.1.call-start = ((), (), s32[]{:S(2)}) async-start(), calls=%async_computation.17 | async-start | bytes 1048576 | tf_op jit(solution)/shard_map/psum | solution.py:278
  456.5 58.9 %reduce-scatter.16.cloned.1.call-start = ((), (), s32[]{:S(2)}) async-start(), calls=%async_computation.16 | async-start | bytes 655360 | tf_op jit(solution)/shard_map/reduce_scatter | solution.py:155
  459.2 120.6 %all-gather.15.cloned.1.call-start = ((), (), s32[]{:S(2)}) async-start(), calls=%async_computation.18 | async-start | bytes 2359296 | tf_op jit(solution)/shard_map/all_gather | solution.py:137
  529.6 194.8 %all-reduce.40.cloned.1.call-start = ((), (), s32[]{:S(2)}) async-start(), calls=%async_computation.19 | async-start | bytes 1048576 | tf_op jit(solution)/shard_map/psum | solution.py:310
  671.4 14.3 collective-permute-start.2
  690.8 74.1 %all-reduce.42.cloned.1.call-start = ((), (), s32[]{:S(2)}) async-start(), calls=%async_computation.20 | async-start | bytes 1048576 | tf_op jit(solution)/shard_map/psum | solution.py:278
  731.3 91.8 %all-gather.17.cloned.1.call-start = ((), (), s32[]{:S(2)}) async-start(), calls=%async_computation.21 | async-start | bytes 2359296 | tf_op jit(solution)/shard_map/all_gather | solution.py:137
  773.3 171.3 %all-reduce.44.cloned.1.call-start = ((), (), s32[]{:S(2)}) async-start(), calls=%async_computation.22 | async-start | bytes 1048576 | tf_op jit(solution)/shard_map/psum | solution.py:310
  884.7 14.0 collective-permute-start.3
  904.8 128.5 %reduce-scatter.20.cloned.1.call-start = ((), (), s32[]{:S(2)}) async-start(), calls=%async_computation.24 | async-start | bytes 4718592 | tf_op jit(solution)/shard_map/reduce_scatter | solution.py:383
  907.6 240.4 %reduce-scatter.26.cloned.1.call-start = ((), (), s32[]{:S(2)}) async-start(), calls=%async_computation.27 | async-start | bytes 6488064 | tf_op jit(solution)/shard_map/reduce_scatter | solution.py:386
  912.7 349.8 %reduce-scatter.22.cloned.1.call-start = ((), (), s32[]{:S(2)}) async-start(), calls=%async_computation.25 | async-start | bytes 6488064 | tf_op jit(solution)/shard_map/reduce_scatter | solution.py:384
  917.8 459.2 %reduce-scatter.24.cloned.1.call-start = ((), (), s32[]{:S(2)}) async-start(), calls=%async_computation.26 | async-start | bytes 6488064 | tf_op jit(solution)/shard_map/reduce_scatter | solution.py:385
  922.8 665.1 %reduce-scatter.18.cloned.1.call-start = ((), (), s32[]{:S(2)}) async-start(), calls=%async_computation.23 | async-start | bytes 14155776 | tf_op jit(solution)/shard_map/reduce_scatter | solution.py:382
  (180 other events, 2248.9 us)
Sparse Core Ops, SparseCore 0:
  70.5 42.4 all-gather.6
  115.7 47.7 all-gather.8
  187.0 20.1 reduce-scatter.9
  219.2 22.1 reduce-scatter.11
  307.1 41.8 all-gather.10
  351.5 47.7 all-gather.12
  423.7 20.1 reduce-scatter.13
  456.6 33.9 all-reduce.37
  493.7 21.7 reduce-scatter.15
  529.8 50.0 all-gather.14
  690.9 33.4 all-reduce.39
  731.4 33.4 all-reduce.41
  773.4 49.6 all-gather.16
  904.9 34.1 all-reduce.43
  943.2 90.0 reduce-scatter.19
  1037.3 110.6 reduce-scatter.25
  1152.1 110.3 reduce-scatter.21
  1266.6 110.3 reduce-scatter.23
  1381.2 206.7 reduce-scatter.17
where the time goes:
time: 1610 us; the launch traced here: 1590 us
  waiting for transfers between devices  1020 us (63%)
  other arithmetic  197 us (12%)
  matrix products  162 us (10%)
  local copies, waits for them, and re-layouts  107 us (7%)
  blocking collectives  72.1 us (4%)
  between operations  16.9 us (1%)
    reduce_scatter x1, waiting for transfers between devices, body(): lax.psum_scatter(large_stack[0], 'seq', scatter_dimension=1, tiled=True)  211 us
    another operation x32, other arithmetic, span_step(): lax.linalg.triangular_solve(system, right_side, left_side=True, lower=True)  122 us
    reduce_scatter x1, waiting for transfers between devices, body(): lax.psum_scatter(large_stack[4], 'seq', scatter_dimension=2, tiled=True)  115 us
    reduce_scatter x1, waiting for transfers between devices, body(): lax.psum_scatter(large_stack[3], 'seq', scatter_dimension=1, tiled=True)  115 us
    reduce_scatter x1, waiting for transfers between devices, body(): lax.psum_scatter(large_stack[2], 'seq', scatter_dimension=1, tiled=True)  114 us
    all_gather x2, waiting for transfers between devices, state_prefix(): lax.all_gather(offset, 'seq', axis=0, tiled=True)  101 us
    all_gather x2, waiting for transfers between devices, state_prefix(): lax.all_gather(transfer, 'seq', axis=0, tiled=True)  82.9 us
    reduce_scatter x4, waiting for transfers between devices, head_total(): lax.psum_scatter(partial_sum, 'head', scatter_dimension=1, tiled=True)  78.4 us
  transfers between devices with their start and end apart: 23, of which 22 were waited for; matrix products, arithmetic and copies ran while one was open for 8% of the time, Pallas kernels for 0%

commit v1 on v0

--- a/solution.py
+++ b/solution.py
@@ -12,6 +12,22 @@
 norm_eps = 1e-06
 gate_unit = 1.0 / 1048576.0
 beta_unit = 1.0 / 1024.0
+
+
+def gather_around(x, axis, dim):
+    ways, here, lap = (lax.axis_size(axis), lax.axis_index(axis), x.shape[dim])
+    shape = [n * ways if d == dim else n for d, n in enumerate(x.shape)]
+    full = lax.dynamic_update_slice_in_dim(jnp.zeros(shape, x.dtype), x, here * lap, axis=dim)
+    going_up = going_down = x
+    for far in range(1, ways // 2 + 1):
+        going_up = lax.ppermute(going_up, axis, [(d, (d + 1) % ways) for d in range(ways)])
+        full = lax.dynamic_update_slice_in_dim(full, going_up, (here - far) % ways * lap, axis=dim)
+        if 2 * far < ways:
+            going_down = lax.ppermute(going_down, axis, [(d, (d - 1) % ways) for d in range(ways)])
+            full = lax.dynamic_update_slice_in_dim(
+                full, going_down, (here + far) % ways * lap, axis=dim
+            )
+    return full
 
 
 def from_behind(array, axis, by):
@@ -115,7 +131,7 @@
 def state_prefix(transfer, offset):
     all_transfer, all_offset = (
         lax.all_gather(transfer, "seq", axis=0, tiled=True),
-        lax.all_gather(offset, "seq", axis=0, tiled=True),
+        gather_around(offset, "seq", 0),
     )
     devices = lax.axis_size("seq")
     position = lax.axis_index("seq")

time: 1610 us -> 1560 us (0.969)
  waiting for transfers between devices: 1020 us -> 875 us
  starting transfers between devices: 13.3 us -> 55 us
  local copies, waits for them, and re-layouts: 107 us -> 148 us
    all_gather x2 -> x0, waiting for transfers between devices: 101 us -> none  [state_prefix(): lax.all_gather(offset, 'seq', axis=0, tiled=True)]
    all_gather x2, waiting for transfers between devices: 82.9 us -> 0.01 us  [state_prefix(): lax.all_gather(transfer, 'seq', axis=0, tiled=True)]
    ppermute x0 -> x14, waiting for transfers between devices: none -> 54 us  [the longest x8 44.6 us: gather_around(): lax.ppermute(going_up, axis, [(d, (d + 1) % ways) for d in range(ways)])]
    ppermute x0 -> x14, starting transfers between devices: none -> 41.9 us  [the longest x6 27.3 us: gather_around(): lax.ppermute(going_down, axis, [(d, (d - 1) % ways) for d in range(ways)])]
    dynamic_slice x32 -> x0, local copies, waits for them, and re-layouts: 17.7 us -> none  [advance(): offsets_all[index_now]]
  transfers between devices with their start and end apart: 23 -> 35, of which waited for: 22 -> 29; matrix products, arithmetic and copies ran while one was open for 8% -> 11% of each run, Pallas kernels for 0% -> 0%
where the time goes in v1:
time: 1560 us; the launch traced here: 1540 us
  waiting for transfers between devices  875 us (56%)
  other arithmetic  209 us (13%)
  matrix products  167 us (11%)
  local copies, waits for them, and re-layouts  148 us (9%)
  blocking collectives  72.2 us (5%)
  starting transfers between devices  55 us (4%)
  between operations  16.6 us (1%)
    reduce_scatter x1, waiting for transfers between devices, body(): lax.psum_scatter(large_stack[0], 'seq', scatter_dimension=1, tiled=True)  211 us
    another operation x32, other arithmetic, span_step(): lax.linalg.triangular_solve(system, right_side, left_side=True, lower=True)  122 us
    reduce_scatter x1, waiting for transfers between devices, body(): lax.psum_scatter(large_stack[4], 'seq', scatter_dimension=2, tiled=True)  115 us
    reduce_scatter x1, waiting for transfers between devices, body(): lax.psum_scatter(large_stack[3], 'seq', scatter_dimension=1, tiled=True)  115 us
    reduce_scatter x1, waiting for transfers between devices, body(): lax.psum_scatter(large_stack[2], 'seq', scatter_dimension=1, tiled=True)  114 us
    reduce_scatter x4, waiting for transfers between devices, head_total(): lax.psum_scatter(partial_sum, 'head', scatter_dimension=1, tiled=True)  77.9 us
    psum x2, waiting for transfers between devices, layer_backward(): grad_normed_two = lax.psum(ffn_partial, 'head')  61.7 us
    reduce_scatter x1, waiting for transfers between devices, body(): lax.psum_scatter(large_stack[1], 'seq', scatter_dimension=2, tiled=True)  46.8 us
  transfers between devices with their start and end apart: 35, of which 29 were waited for; matrix products, arithmetic and copies ran while one was open for 11% of the time, Pallas kernels for 0%

profile of v1, /device:TPU:0, one launch (start us, length us, event | category | flops | bytes accessed | tf_op | source)
XLA Modules:
  0.0 1544.8 jit_solution(12813251816766755993)
XLA Ops:
  41.0 29.7 %while.210 = (s32[]{:T(128)}, f32[2,384,128]{2,1,0:T(8,128)S(1)}, f32[2,64,2,384]{3,1,0,2:T(8,128)S(1)}, f32[2,64,2]{1,2,0:T(2,128)}, f32[2,64,2]{1,2,0:T(2,128)...) while((s32[]{:T(128)}, f32[2,384,128]{2,1,0:T(8,128)S(1)}, ...), condition=%wide.region_5.7_spmd, body=%wide.region_3.6_spmd.sunk | while | flops 340353152 | bytes 4627117 | solution.py:117
  42.6 9.8 custom-call.34
  57.5 9.8 custom-call.34
  107.4 11.1 collective-permute-done.5
  131.3 12.1 while.216
  146.8 20.1 %reduce-scatter.10.cloned.1.call-done = f32[128,256]{1,0:T(8,128)} async-done(((f32[128,1024]{1,0:T(8,128)}), f32[128,256]{1,0:T(8,128)}) %reduce-scatter.10.cloned.1.call-update) | async-done | bytes 131088 | tf_op jit(solution)/shard_map/reduce_scatter | solution.py:171
  184.0 17.5 %reduce-scatter.12.cloned.1.call-done = f32[128,256]{1,0:T(8,128)} async-done(((f32[128,1024]{1,0:T(8,128)}), f32[128,256]{1,0:T(8,128)}) %reduce-scatter.12.cloned.1.call-update) | async-done | bytes 131088 | tf_op jit(solution)/shard_map/reduce_scatter | solution.py:171
  239.2 33.0 %while.211 = (s32[]{:T(128)}, f32[2,384,128]{2,1,0:T(8,128)S(1)}, f32[2,64,2,384]{3,1,0,2:T(8,128)}, f32[2,64,2]{1,2,0:T(2,128)}, f32[2,64,2]{1,2,0:T(2,128)}, /...) while((s32[]{:T(128)}, f32[2,384,128]{2,1,0:T(8,128)S(1)}, ...), condition=%wide.region_17.19_spmd, body=%wide.region_15.18_spmd.sunk | while | flops 340353152 | bytes 4627117 | solution.py:117
  240.8 9.8 custom-call.35
  333.1 12.1 while.217
  354.4 17.3 %reduce-scatter.14.cloned.1.call-done = f32[128,256]{1,0:T(8,128)} async-done(((f32[128,1024]{1,0:T(8,128)}), f32[128,256]{1,0:T(8,128)}) %reduce-scatter.14.cloned.1.call-update) | async-done | bytes 131088 | tf_op jit(solution)/shard_map/reduce_scatter | solution.py:171
  389.5 28.2 %all-reduce.38.cloned.1.call-done = f32[128,1024]{1,0:T(8,128)} async-done(((f32[128,1024]{1,0:T(8,128)}), f32[128,1024]{1,0:T(8,128)}) %all-reduce.38.cloned.1.call-update) | async-done | bytes 524304 | tf_op jit(solution)/shard_map/psum | solution.py:294
  419.5 23.0 %reduce-scatter.16.cloned.1.call-done = f32[128,256]{1,0:T(8,128)} async-done(((f32[128,1024]{1,0:T(8,128)}), f32[128,256]{1,0:T(8,128)}) %reduce-scatter.16.cloned.1.call-update) | async-done | bytes 131088 | tf_op jit(solution)/shard_map/reduce_scatter | solution.py:171
  463.7 41.5 %while.214 = (s32[]{:T(128)}, f32[2,256,128]{2,1,0:T(8,128)S(1)}, f32[2,2,64,64]{3,2,1,0:T(8,128)}, f32[2,64,2,1]{1,2,3,0:T(2,128)}, f32[2,64,2,1]{1,2,3,0:T(2,1...) while((s32[]{:T(128)}, f32[2,256,128]{2,1,0:T(8,128)S(1)}, ...), condition=%wide.region_31.34_spmd.clone.clone, body=%wide.region_29.33_spmd.clone.clone.sunk | while | flops 164024704 | bytes 3922773 | solution.py:117
  471.0 9.9 custom-call.38
  506.0 32.4 %while.218 = (s32[]{:T(128)}, f32[2,256,128]{1,2,0:T(8,128)}, s32[]{:T(128)}, f32[8,2,128,128]{3,2,1,0:T(8,128)}, f32[8,2,256,128]{3,2,1,0:T(8,128)}, /*index=5*/s32[]{:T(128)}, s32[]{:T(128)}, s32[]{:T(128)}, s32[]{:T(128)}) while((s32[]{:T(128)}, f32[2,256,128]{1,2,0:T(8,128)}, s32[]{:T(128)}, f32[8,2,128,128]{3,2,1,0:T(8,128)}, ...), condition=%wide.region_28.30_spmd.clone, body=%wide.region_27.29_spmd.clone.sunk | while | flops 100925448 | bytes 2754729 | solution.py:166
  541.6 49.3 %while.212 = (s32[]{:T(128)}, f32[2,256,128]{2,1,0:T(8,128)S(1)}, f32[2,64,2,128]{3,1,0,2:T(8,128)}, f32[2,64,2,128]{3,1,0,2:T(8,128)}, f32[2,64,2,256]{3,1,0,2:...) while((s32[]{:T(128)}, f32[2,256,128]{2,1,0:T(8,128)S(1)}, ...), condition=%wide.region_33.38_spmd.clone, body=%wide.region_32.37_spmd.clone.sunk | while | flops 485101568 | bytes 12066977 | solution.py:117
  606.6 13.4 collective-permute-done.16
  624.5 34.0 %all-reduce.40.cloned.1.call-done = f32[128,1024]{1,0:T(8,128)} async-done(((f32[128,1024]{1,0:T(8,128)}), f32[128,1024]{1,0:T(8,128)}) %all-reduce.40.cloned.1.call-update) | async-done | bytes 524304 | tf_op jit(solution)/shard_map/psum | solution.py:326
  665.8 33.5 %all-reduce.42.cloned.1.call-done = f32[128,1024]{1,0:T(8,128)} async-done(((f32[128,1024]{1,0:T(8,128)}), f32[128,1024]{1,0:T(8,128)}) %all-reduce.42.cloned.1.call-update) | async-done | bytes 524304 | tf_op jit(solution)/shard_map/psum | solution.py:294
  714.4 39.3 %while.215 = (s32[]{:T(128)}, f32[2,256,128]{2,1,0:T(8,128)S(1)}, f32[2,2,64,64]{3,2,1,0:T(8,128)S(1)}, f32[2,64,2,1]{1,2,3,0:T(2,128)S(1)}, f32[2,64,2,1]{1,2,3...) while((s32[]{:T(128)}, f32[2,256,128]{2,1,0:T(8,128)S(1)}, ...), condition=%wide.region_45.50_spmd.clone.clone, body=%wide.region_43.49_spmd.clone.clone.sunk | while | flops 164024704 | bytes 3956617 | solution.py:117
  721.4 9.9 custom-call.39
  741.0 9.8 custom-call.39
  758.2 19.6 %while.219 = (s32[]{:T(128)}, f32[2,256,128]{1,2,0:T(8,128)S(1)}, s32[]{:T(128)}, f32[8,2,128,128]{3,2,1,0:T(8,128)}, f32[8,2,256,128]{3,2,1,0:T(8,128)}, /*index=5*/s32[]{:T(128)}, s32[]{:T(128)}, s32[]{:T(128)}, s32[]{:T(128)}) while((s32[]{:T(128)}, f32[2,256,128]{1,2,0:T(8,128)S(1)}, s32[]{:T(128)}, ...), condition=%wide.region_42.47_spmd.clone, body=%wide.region_41.46_spmd.clone.sunk | while | flops 100925448 | bytes 2754729 | solution.py:166
  779.4 44.9 %while.213 = (s32[]{:T(128)}, f32[2,256,128]{2,1,0:T(8,128)S(1)}, f32[2,64,2,128]{3,1,0,2:T(8,128)}, f32[2,64,2,128]{3,1,0,2:T(8,128)S(1)}, f32[2,64,2,256]{3,1,...) while((s32[]{:T(128)}, f32[2,256,128]{2,1,0:T(8,128)S(1)}, ...), condition=%wide.region_47.52_spmd.clone, body=%wide.region_46.51_spmd.clone.sunk | while | flops 485101568 | bytes 7307113 | solution.py:117
  836.8 12.0 collective-permute-done.17
  896.2 38.5 %all-reduce.31 = (f32[2,1024]{1,0:T(2,128)}, f32[2,4,1024]{2,1,0:T(4,128)}, f32[2,256]{1,0:T(2,128)}, f32[2,1024]{1,0:T(2,128)}) all-reduce(f32[2,1024]{1,0:T(2,128)S(1)} %pad_maximum_fusion.8, f32[2,4,1024]{2,1,0:T(4,128)S(1)} %pad_maximum_fusion.7, ...), channel_id=1, replica_groups=mesh['seq'=8,'head'=4] {'seq'}, use_global_device_ids=true, to_apply=%region_54.59 | all-reduce | flops 12800 | bytes 102400 | tf_op jit(solution)/shard_map/psum | solution.py:410
  936.7 46.8 %reduce-scatter.20.cloned.1.call-done = f32[2,512,128]{2,1,0:T(8,128)} async-done(((f32[2,512,1024]{2,1,0:T(8,128)}), f32[2,512,128]{2,1,0:T(8,128)}) %reduce-scatter.20.cloned.1.call-update) | async-done | bytes 524304 | tf_op jit(solution)/shard_map/reduce_scatter | solution.py:399
  983.5 114.8 %reduce-scatter.26.cloned.1.call-done = f32[2,704,128]{2,1,0:T(8,128)} async-done(((f32[2,704,1024]{2,1,0:T(8,128)}), f32[2,704,128]{2,1,0:T(8,128)}) %reduce-scatter.26.cloned.1.call-update) | async-done | bytes 720912 | tf_op jit(solution)/shard_map/reduce_scatter | solution.py:402
  1098.3 114.5 %reduce-scatter.22.cloned.1.call-done = f32[2,128,704]{1,2,0:T(8,128)} async-done(((f32[2,1024,704]{1,2,0:T(8,128)}), f32[2,128,704]{1,2,0:T(8,128)}) %reduce-scatter.22.cloned.1.call-update) | async-done | bytes 720912 | tf_op jit(solution)/shard_map/reduce_scatter | solution.py:400
  1212.8 114.5 %reduce-scatter.24.cloned.1.call-done = f32[2,128,704]{1,2,0:T(8,128)} async-done(((f32[2,1024,704]{1,2,0:T(8,128)}), f32[2,128,704]{1,2,0:T(8,128)}) %reduce-scatter.24.cloned.1.call-update) | async-done | bytes 720912 | tf_op jit(solution)/shard_map/reduce_scatter | solution.py:401
  1327.3 210.8 %reduce-scatter.18.cloned.1.call-done = f32[2,128,1536]{2,1,0:T(8,128)} async-done(((f32[2,1024,1536]{2,1,0:T(8,128)}), f32[2,128,1536]{2,1,0:T(8,128)}) %reduce-scatter.18.cloned.1.call-update) | async-done | bytes 1572880 | tf_op jit(solution)/shard_map/reduce_scatter | solution.py:398
  (1079 shorter events, 616.7 us)
Async XLA Ops:
  7.2 124.1 %all-gather.5.cloned.1.call-start = ((), (), s32[]{:S(2)}) async-start(), calls=%async_computation.9 | async-start | bytes 1179648 | tf_op jit(solution)/shard_map/all_gather | solution.py:133
  20.6 16.1 %collective-permute-start = (f32[3,1024]{0,1:T(8,128)S(1)}, f32[3,1024]{0,1:T(8,128)S(1)}, u32[]{:S(2)}, u32[]{:S(2)}) collective-permute-start(f32[3,1024]{0,1:T(8,128)S(1)} %copy.568), channel_id=1, source_target_pairs={{0,4},{4,8},{8,12},{12,16},{16,20},{20,24},{24,28},{1,5},{5,9},{9,... | collective-permute-start | bytes 36872 | tf_op jit(solution)/shard_map/ppermute | solution.py:36
  71.5 95.4 %reduce-scatter.10.cloned.1.call-start = ((), (), s32[]{:S(2)}) async-start(), calls=%async_computation.10 | async-start | bytes 655360 | tf_op jit(solution)/shard_map/reduce_scatter | solution.py:171
  77.1 13.1 collective-permute-start.1
  81.8 21.1 %collective-permute-start.4 = (f32[2,256,128]{2,1,0:T(8,128)S(1)}, f32[2,256,128]{2,1,0:T(8,128)S(1)}, u32[]{:S(2)}, u32[]{:S(2)}) collective-permute-start(f32[2,256,128]{2,1,0:T(8,128)S(1)} %collective-permute-done.2), channel_id=1, source_target_pairs={{0,28},{4,0},{8,4},{12,8},{16,12},{20,16},{24,20},{28,24},{1,29},{... | collective-permute-start | bytes 786440 | tf_op jit(solution)/shard_map/ppermute | solution.py:26
  100.0 18.5 %collective-permute-start.5 = (f32[2,256,128]{2,1,0:T(8,128)S(1)}, f32[2,256,128]{2,1,0:T(8,128)S(1)}, u32[]{:S(2)}, u32[]{:S(2)}) collective-permute-start(f32[2,256,128]{2,1,0:T(8,128)S(1)} %collective-permute-done.3), channel_id=1, source_target_pairs={{0,4},{4,8},{8,12},{12,16},{16,20},{20,24},{24,28},{28,0},{1,5},{5... | collective-permute-start | bytes 786440 | tf_op jit(solution)/shard_map/ppermute | solution.py:23
  102.9 21.2 %collective-permute-start.6 = (f32[2,256,128]{2,1,0:T(8,128)S(1)}, f32[2,256,128]{2,1,0:T(8,128)S(1)}, u32[]{:S(2)}, u32[]{:S(2)}) collective-permute-start(f32[2,256,128]{2,1,0:T(8,128)S(1)} %collective-permute-done.4), channel_id=1, source_target_pairs={{0,28},{4,0},{8,4},{12,8},{16,12},{20,16},{24,20},{28,24},{1,29},{... | collective-permute-start | bytes 786440 | tf_op jit(solution)/shard_map/ppermute | solution.py:26
  146.7 54.9 %reduce-scatter.12.cloned.1.call-start = ((), (), s32[]{:S(2)}) async-start(), calls=%async_computation.11 | async-start | bytes 655360 | tf_op jit(solution)/shard_map/reduce_scatter | solution.py:171
  179.2 153.9 %all-gather.7.cloned.1.call-start = ((), (), s32[]{:S(2)}) async-start(), calls=%async_computation.12 | async-start | bytes 1179648 | tf_op jit(solution)/shard_map/all_gather | solution.py:133
  213.3 15.4 collective-permute-start.8
  272.9 98.8 %reduce-scatter.14.cloned.1.call-start = ((), (), s32[]{:S(2)}) async-start(), calls=%async_computation.13 | async-start | bytes 655360 | tf_op jit(solution)/shard_map/reduce_scatter | solution.py:171
  273.0 14.8 collective-permute-start.9
  275.5 15.2 collective-permute-start.10
  287.7 12.7 collective-permute-start.11
  290.7 14.0 collective-permute-start.12
  300.4 17.8 %collective-permute-start.13 = (f32[2,256,128]{2,1,0:T(8,128)}, f32[2,256,128]{2,1,0:T(8,128)}, u32[]{:S(2)}, u32[]{:S(2)}) collective-permute-start(f32[2,256,128]{2,1,0:T(8,128)} %collective-permute-done.11), channel_id=1, source_target_pairs={{0,4},{4,8},{8,12},{12,16},{16,20},{20,24},{24,28},{28,0},{1,5},{5... | collective-permute-start | bytes 786440 | tf_op jit(solution)/shard_map/ppermute | solution.py:23
  304.7 19.9 %collective-permute-start.14 = (f32[2,256,128]{2,1,0:T(8,128)}, f32[2,256,128]{2,1,0:T(8,128)}, u32[]{:S(2)}, u32[]{:S(2)}) collective-permute-start(f32[2,256,128]{2,1,0:T(8,128)} %collective-permute-done.12), channel_id=1, source_target_pairs={{0,28},{4,0},{8,4},{12,8},{16,12},{20,16},{24,20},{28,24},{1,29},{... | collective-permute-start | bytes 786440 | tf_op jit(solution)/shard_map/ppermute | solution.py:26
  318.3 13.0 collective-permute-start.15
  351.5 66.2 %all-reduce.38.cloned.1.call-start = ((), (), s32[]{:S(2)}) async-start(), calls=%async_computation.15 | async-start | bytes 1048576 | tf_op jit(solution)/shard_map/psum | solution.py:294
  383.6 59.0 %reduce-scatter.16.cloned.1.call-start = ((), (), s32[]{:S(2)}) async-start(), calls=%async_computation.14 | async-start | bytes 655360 | tf_op jit(solution)/shard_map/reduce_scatter | solution.py:171
  386.3 119.8 %all-gather.9.cloned.1.call-start = ((), (), s32[]{:S(2)}) async-start(), calls=%async_computation.16 | async-start | bytes 2359296 | tf_op jit(solution)/shard_map/all_gather | solution.py:153
  455.9 202.5 %all-reduce.40.cloned.1.call-start = ((), (), s32[]{:S(2)}) async-start(), calls=%async_computation.17 | async-start | bytes 1048576 | tf_op jit(solution)/shard_map/psum | solution.py:326
  603.9 16.1 %collective-permute-start.16 = (f32[3,1024]{0,1:T(8,128)}, f32[3,1024]{0,1:T(8,128)S(1)}, u32[]{:S(2)}, u32[]{:S(2)}) collective-permute-start(f32[3,1024]{0,1:T(8,128)} %slice.407), channel_id=1, source_target_pairs={{4,0},{8,4},{12,8},{16,12},{20,16},{24,20},{28,24},{5,1},{9,5},{13... | collective-permute-start | bytes 36872 | tf_op jit(solution)/shard_map/ppermute | solution.py:36
  624.4 74.8 %all-reduce.42.cloned.1.call-start = ((), (), s32[]{:S(2)}) async-start(), calls=%async_computation.18 | async-start | bytes 1048576 | tf_op jit(solution)/shard_map/psum | solution.py:294
  665.6 92.6 %all-gather.11.cloned.1.call-start = ((), (), s32[]{:S(2)}) async-start(), calls=%async_computation.19 | async-start | bytes 2359296 | tf_op jit(solution)/shard_map/all_gather | solution.py:153
  708.6 186.3 %all-reduce.44.cloned.1.call-start = ((), (), s32[]{:S(2)}) async-start(), calls=%async_computation.20 | async-start | bytes 1048576 | tf_op jit(solution)/shard_map/psum | solution.py:326
  834.7 14.0 collective-permute-start.17
  855.0 128.5 %reduce-scatter.20.cloned.1.call-start = ((), (), s32[]{:S(2)}) async-start(), calls=%async_computation.22 | async-start | bytes 4718592 | tf_op jit(solution)/shard_map/reduce_scatter | solution.py:399
  857.8 240.5 %reduce-scatter.26.cloned.1.call-start = ((), (), s32[]{:S(2)}) async-start(), calls=%async_computation.25 | async-start | bytes 6488064 | tf_op jit(solution)/shard_map/reduce_scatter | solution.py:402
  862.9 349.9 %reduce-scatter.22.cloned.1.call-start = ((), (), s32[]{:S(2)}) async-start(), calls=%async_computation.23 | async-start | bytes 6488064 | tf_op jit(solution)/shard_map/reduce_scatter | solution.py:400
  868.0 459.3 %reduce-scatter.24.cloned.1.call-start = ((), (), s32[]{:S(2)}) async-start(), calls=%async_computation.24 | async-start | bytes 6488064 | tf_op jit(solution)/shard_map/reduce_scatter | solution.py:401
  873.1 665.0 %reduce-scatter.18.cloned.1.call-start = ((), (), s32[]{:S(2)}) async-start(), calls=%async_computation.21 | async-start | bytes 14155776 | tf_op jit(solution)/shard_map/reduce_scatter | solution.py:398
  (184 other events, 3564.9 us)
Sparse Core Ops, SparseCore 0:
  71.6 56.9 all-gather.4
  146.8 19.9 reduce-scatter.9
  179.3 22.1 reduce-scatter.11
  273.0 56.1 all-gather.6
  351.7 19.9 reduce-scatter.13
  383.7 33.9 all-reduce.37
  420.8 21.7 reduce-scatter.15
  456.0 49.9 all-gather.8
  624.5 33.8 all-reduce.39
  665.7 33.4 all-reduce.41
  708.7 49.4 all-gather.10
  855.1 34.0 all-reduce.43
  893.4 90.0 reduce-scatter.19
  987.6 110.6 reduce-scatter.25
  1102.4 110.3 reduce-scatter.21
  1216.9 110.3 reduce-scatter.23
  1331.3 206.7 reduce-scatter.17
